TPU v7x, 256 devices: a whole 4x4x8 slice. The times are simulated.
256 devices in a mesh: gx: 16 (over z, y_lo), gy: 16 (over y_hi, x, core).
Axes of the slice: x: 4, y: 4 (y_hi: 2, y_lo: 2; y = y_hi * 2 + y_lo), z: 8, core: 2. Of those that a mesh axis runs over, the one named last changes fastest.
Arguments:
- psi: float32 [64, 128, 4096], P(None, 'gx', 'gy'), may hold values from -500 to 500
- potential: float32 [128, 4096], P('gx', 'gy'), may hold values from -2 to 0
Outputs:
- orbitals: float32 [64, 128, 4096], P(None, 'gx', 'gy')
All inputs are finite; a program needn't handle non-finite values.
Results may differ from a plain program's by a relative error of at most 0.0003.
Values sent between devices are 32-bit elements; how exact they have to be, the bound alone decides.
No kernel may reach another device: no remote copies, remote signals or barrier semaphores. Data moves between devices by JAX's collectives and lax.ppermute only.
A program may use at most 64 MiB of HBM per device.

v0:
```python
import jax
import jax.numpy as jnp
from jax import lax
from jax.sharding import PartitionSpec as P

NZ = 64
COEFS = (-205.0 / 72.0, 8.0 / 5.0, -1.0 / 5.0, 8.0 / 315.0, -1.0 / 560.0)
CENTER = 6.5
HALF_WIDTH = 5.5


def padded(array, sides, width):
    for axis, dim in sides:
        size, length = (lax.axis_size(axis), array.shape[dim])
        up = [(i, (i + 1) % size) for i in range(size)]
        down = [(j, i) for i, j in up]
        last = lax.slice_in_dim(array, length - width, length, axis=dim)
        first = lax.slice_in_dim(array, 0, width, axis=dim)
        before = lax.ppermute(last, axis, up)
        after = lax.ppermute(first, axis, down)
        array = jnp.concatenate([before, array, after], axis=dim)
    return array


def along_third(field, depth_index):
    laplace = 3.0 * COEFS[0] * field
    for distance in range(1, 5):
        forward = jnp.where(
            depth_index < NZ - distance,
            jnp.roll(field, -distance, 2),
            jnp.roll(field, NZ - distance, 2),
        )
        behind = jnp.where(
            depth_index >= distance, jnp.roll(field, distance, 2), jnp.roll(field, distance - NZ, 2)
        )
        laplace = laplace + COEFS[distance] * (forward + behind)
    return laplace


def hamiltonian(field, field_pot, depth_index):
    row_count = field.shape[1]
    lane_count = field.shape[2]
    padded_x = padded(field, (("gx", 1),), 4)
    laplace = along_third(field, depth_index)
    padded_y = padded(field, (("gy", 2),), 4 * NZ)
    for distance in range(1, 5):
        laplace = laplace + COEFS[distance] * (
            padded_x[:, 4 + distance : 4 + distance + row_count]
            + padded_x[:, 4 - distance : 4 - distance + row_count]
        )
        ahead_start = (4 + distance) * NZ
        back_start = (4 - distance) * NZ
        laplace = laplace + COEFS[distance] * (
            padded_y[:, :, ahead_start : ahead_start + lane_count]
            + padded_y[:, :, back_start : back_start + lane_count]
        )
    return -0.5 * laplace + field_pot * field


def orthonormal(matrix, ncount):
    local_gram = jnp.dot(matrix, matrix.T, precision=lax.Precision.HIGHEST) / ncount
    total_gram = lax.psum(local_gram, ("gx", "gy"))
    lower_factor = jnp.linalg.cholesky(total_gram)
    return lax.linalg.triangular_solve(lower_factor, matrix, left_side=True, lower=True)


def on_device(psi, potential):
    orbit_count = psi.shape[0]
    row_count = psi.shape[1]
    lane_count = psi.shape[2]
    field_pot = potential.reshape(1, row_count, lane_count)
    depth_index = lax.broadcasted_iota(jnp.int32, (1, 1, lane_count), 2) % NZ
    level_one = (hamiltonian(psi, field_pot, depth_index) - CENTER * psi) / HALF_WIDTH
    second = (
        2.0 * (hamiltonian(level_one, field_pot, depth_index) - CENTER * level_one) / HALF_WIDTH
        - psi
    )
    filtered = (
        2.0 * (hamiltonian(second, field_pot, depth_index) - CENTER * second) / HALF_WIDTH
        - level_one
    )
    matrix = filtered.reshape(orbit_count, row_count * lane_count)
    ncount = float(row_count * lane_count * lax.axis_size("gx") * lax.axis_size("gy"))
    first_pass = orthonormal(matrix, ncount)
    final_pass = orthonormal(first_pass, ncount)
    return final_pass.reshape(orbit_count, row_count, lane_count)


def solution(mesh):
    in_specs = (P(None, "gx", "gy"), P("gx", "gy"))
    out_specs = P(None, "gx", "gy")
    return jax.shard_map(
        on_device, mesh=mesh, in_specs=in_specs, out_specs=out_specs, check_vma=False
    )
```

profile of v0, /device:TPU:1, one launch (start us, length us, event | category | flops | bytes accessed | tf_op | source)
XLA Modules:
  0.0 262.9 jit_solution(8503108184494606311)
XLA Ops:
  0.0 2.6 collective-permute-start.3
  3.2 1.3 fusion.198
  4.5 6.0 %collective-permute-start = (f32[64,4,256]{2,1,0:T(4,128)S(1)}, f32[64,4,256]{2,1,0:T(4,128)S(1)}, u32[]{:S(2)}, u32[]{:S(2)}) collective-permute-start(f32[64,4,256]{2,1,0:T(4,128)S(1)} %get-tuple-element.112), channel_id=1, source_target_pairs={{16,0},{32,16},{48,32},{64,48},{80,64},{96,80},{112,96},{128,112},... | collective-permute-start | bytes 786440 | tf_op jit(solution)/shard_map/ppermute | solution.py:20
  14.2 6.1 %collective-permute-done = f32[64,4,256]{2,1,0:T(4,128)S(1)} collective-permute-done((f32[64,4,256]{2,1,0:T(4,128)S(1)}, f32[64,4,256]{2,1,0:T(4,128)S(1)}, u32[]{:S(2)}, u32[]{:S(2)}) %collective-permute-start) | collective-permute-done | bytes 262176 | tf_op jit(solution)/shard_map/ppermute | solution.py:20
  20.4 3.0 %collective-permute-done.1 = f32[64,4,256]{2,1,0:T(4,128)S(1)} collective-permute-done((f32[64,4,256]{2,1,0:T(4,128)S(1)}, f32[64,4,256]{2,1,0:T(4,128)S(1)}, u32[]{:S(2)}, u32[]{:S(2)}) %collective-permute-start.1) | collective-permute-done | bytes 262176 | tf_op jit(solution)/shard_map/ppermute | solution.py:19
  23.4 3.3 %broadcast_multiply_fusion = (f32[64,8,256]{2,1,0:T(8,128)S(1)}, f32[64,8,256]{2,1,0:T(8,128)S(1)}) fusion(f32[64,8,256]{2,1,0:T(8,128)S(1)} %copy-done, f32[8,256]{1,0:T(8,128)S(1)} %copy-done.1, f32[64,8,256]{2,1,0:T(8,128)S(1)} %collective-permute-done.2, f32[64,8,256]{2,1,0:T(8,128)S(1)} %collective-permute-done.3, ...), kind=kLoop, calls=%fused_computation.221 | loop fusion | flops 9306112 | bytes 16525312 | tf_op jit(solution)/shard_map/div | solution.py:73
  29.2 1.5 collective-permute-start.6
  31.0 6.1 %collective-permute-start.4 = (f32[64,4,256]{2,1,0:T(4,128)S(1)}, f32[64,4,256]{2,1,0:T(4,128)S(1)}, u32[]{:S(2)}, u32[]{:S(2)}) collective-permute-start(f32[64,4,256]{2,1,0:T(4,128)S(1)} %get-tuple-element.75), channel_id=1, source_target_pairs={{16,0},{32,16},{48,32},{64,48},{80,64},{96,80},{112,96},{128,112},... | collective-permute-start | bytes 786440 | tf_op jit(solution)/shard_map/ppermute | solution.py:20
  37.5 3.5 %collective-permute-done.4 = f32[64,4,256]{2,1,0:T(4,128)S(1)} collective-permute-done((f32[64,4,256]{2,1,0:T(4,128)S(1)}, f32[64,4,256]{2,1,0:T(4,128)S(1)}, u32[]{:S(2)}, u32[]{:S(2)}) %collective-permute-start.4) | collective-permute-done | bytes 262176 | tf_op jit(solution)/shard_map/ppermute | solution.py:20
  41.0 10.6 %collective-permute-done.5 = f32[64,4,256]{2,1,0:T(4,128)S(1)} collective-permute-done((f32[64,4,256]{2,1,0:T(4,128)S(1)}, f32[64,4,256]{2,1,0:T(4,128)S(1)}, u32[]{:S(2)}, u32[]{:S(2)}) %collective-permute-start.5) | collective-permute-done | bytes 262176 | tf_op jit(solution)/shard_map/ppermute | solution.py:19
  51.6 3.7 %fusion.33 = f32[64,8,256]{2,1,0:T(8,128)S(1)} fusion(f32[64,8,256]{2,1,0:T(8,128)S(1)} %copy-done, f32[64,8,256]{2,1,0:T(8,128)S(1)} %collective-permute-done.7, f32[64,8,256]{2,1,0:T(8,128)S(1)} %get-tuple-element.6, f32[64,8,256]{2,1,0:T(8,128)S(1)} %collective-permute-done.6, f32[64,4,256]{2,1,0:T(4,128)S(1)} %collective-permute-done.5, ...), kind=kLoop, calls=%fused_computation.81 | loop fusion | flops 10747904 | bytes 12068864 | tf_op jit(solution)/shard_map/sub | solution.py:75
  56.6 1.3 collective-permute-start.10
  59.5 4.7 %collective-permute-start.8 = (f32[64,4,256]{2,1,0:T(4,128)S(1)}, f32[64,4,256]{2,1,0:T(4,128)S(1)}, u32[]{:S(2)}, u32[]{:S(2)}) collective-permute-start(f32[64,4,256]{2,1,0:T(4,128)S(1)} %get-tuple-element.41), channel_id=1, source_target_pairs={{16,0},{32,16},{48,32},{64,48},{80,64},{96,80},{112,96},{128,112},... | collective-permute-start | bytes 786440 | tf_op jit(solution)/shard_map/ppermute | solution.py:20
  64.7 3.0 %collective-permute-done.8 = f32[64,4,256]{2,1,0:T(4,128)S(1)} collective-permute-done((f32[64,4,256]{2,1,0:T(4,128)S(1)}, f32[64,4,256]{2,1,0:T(4,128)S(1)}, u32[]{:S(2)}, u32[]{:S(2)}) %collective-permute-start.8) | collective-permute-done | bytes 262176 | tf_op jit(solution)/shard_map/ppermute | solution.py:20
  67.6 12.3 %collective-permute-done.9 = f32[64,4,256]{2,1,0:T(4,128)S(1)} collective-permute-done((f32[64,4,256]{2,1,0:T(4,128)S(1)}, f32[64,4,256]{2,1,0:T(4,128)S(1)}, u32[]{:S(2)}, u32[]{:S(2)}) %collective-permute-start.9) | collective-permute-done | bytes 262176 | tf_op jit(solution)/shard_map/ppermute | solution.py:19
  80.0 3.7 %fusion.13 = f32[64,8,256]{2,1,0:T(8,128)S(1)} fusion(f32[64,8,256]{2,1,0:T(8,128)S(1)} %collective-permute-done.11, f32[64,8,256]{2,1,0:T(8,128)S(1)} %fusion.33, f32[64,8,256]{2,1,0:T(8,128)S(1)} %collective-permute-done.10, f32[64,4,256]{2,1,0:T(4,128)S(1)} %collective-permute-done.9, f32[64,4,256]{2,1,0:T(4,128)S(1)} %collective-permute-done.8, ...), kind=kLoop, calls=%fused_computation.61 | loop fusion | flops 10878976 | bytes 11544576 | tf_op jit(solution)/shard_map/sub | solution.py:79
  83.7 0.7 fusion
  84.4 78.3 %psum.14 = f32[64,64]{0,1:T(8,128)S(1)} all-reduce(f32[64,64]{0,1:T(8,128)S(1)} %fusion), channel_id=1, replica_groups=mesh['gx'=16,'gy'=16] {'gx','gy'}, use_global_device_ids=true, to_apply=%region_0.1 | all-reduce | flops 4096 | bytes 32768 | tf_op jit(solution)/shard_map/psum | solution.py:62
  162.9 5.8 %cholesky.44 = f32[64,64]{1,0:T(8,128)S(1)} custom-call(f32[64,64]{1,0:T(8,128)S(1)} %fusion.144), custom_call_target="Cholesky" | custom-call | tf_op jit(solution)/shard_map/jit(cholesky)/cholesky | solution.py:63
  170.0 4.9 %custom-call.6 = f32[1,64,64]{1,2,0:T(8,128)S(1)} custom-call(f32[1,64,64]{2,1,0:T(8,128)S(1)} %fusion.137), custom_call_target="InvertDiagBlocksLowerTriangular" | custom-call | tf_op jit(solution)/shard_map/triangular_solve/custom-call.0 | solution.py:64
  176.3 72.7 %psum.15 = f32[64,64]{0,1:T(8,128)S(1)} all-reduce(f32[64,64]{0,1:T(8,128)S(1)} %convolution_multiply_fusion), channel_id=1, replica_groups=mesh['gx'=16,'gy'=16] {'gx','gy'}, use_global_device_ids=true, to_apply=%region_3.6 | all-reduce | flops 4096 | bytes 32768 | tf_op jit(solution)/shard_map/psum | solution.py:62
  249.2 5.8 %cholesky.55 = f32[64,64]{1,0:T(8,128)S(1)} custom-call(f32[64,64]{1,0:T(8,128)S(1)} %fusion.141), custom_call_target="Cholesky" | custom-call | tf_op jit(solution)/shard_map/jit(cholesky)/cholesky | solution.py:63
  256.4 4.9 %custom-call.7 = f32[1,64,64]{1,2,0:T(8,128)S(1)} custom-call(f32[1,64,64]{2,1,0:T(8,128)S(1)} %fusion.138), custom_call_target="InvertDiagBlocksLowerTriangular" | custom-call | tf_op jit(solution)/shard_map/triangular_solve/custom-call.0 | solution.py:64
  261.9 1.0 copy.13
  (89 shorter events, 15.5 us)
Async XLA Ops:
  0.0 10.6 %copy-start = (f32[64,8,256]{2,1,0:T(8,128)S(1)}, f32[64,8,256]{2,1,0:T(8,128)}, u32[]{:S(2)}) copy-start(f32[64,8,256]{2,1,0:T(8,128)} %param.5) | copy-start | bytes 1572868
  0.0 13.9 %collective-permute-start.3 = (f32[64,8,256]{2,1,0:T(8,128)}, f32[64,8,256]{2,1,0:T(8,128)S(1)}, u32[]{:S(2)}, u32[]{:S(2)}) collective-permute-start(f32[64,8,256]{2,1,0:T(8,128)} %param.5), channel_id=1, source_target_pairs={{0,1},{1,2},{2,3},{3,4},{4,5},{5,6},{6,7},{7,8},{8,9},{9,10},{10,1... | collective-permute-start | bytes 1572872 | tf_op jit(solution)/shard_map/ppermute | solution.py:19
  2.6 17.7 %collective-permute-start.2 = (f32[64,8,256]{2,1,0:T(8,128)}, f32[64,8,256]{2,1,0:T(8,128)S(1)}, u32[]{:S(2)}, u32[]{:S(2)}) collective-permute-start(f32[64,8,256]{2,1,0:T(8,128)} %param.5), channel_id=1, source_target_pairs={{1,0},{2,1},{3,2},{4,3},{5,4},{6,5},{7,6},{8,7},{9,8},{10,9},{11,1... | collective-permute-start | bytes 1572872 | tf_op jit(solution)/shard_map/ppermute | solution.py:20
  4.5 15.7 %collective-permute-start = (f32[64,4,256]{2,1,0:T(4,128)S(1)}, f32[64,4,256]{2,1,0:T(4,128)S(1)}, u32[]{:S(2)}, u32[]{:S(2)}) collective-permute-start(f32[64,4,256]{2,1,0:T(4,128)S(1)} %get-tuple-element.112), channel_id=1, source_target_pairs={{16,0},{32,16},{48,32},{64,48},{80,64},{96,80},{112,96},{128,112},... | collective-permute-start | bytes 786440 | tf_op jit(solution)/shard_map/ppermute | solution.py:20
  10.6 12.9 %collective-permute-start.1 = (f32[64,4,256]{2,1,0:T(4,128)S(1)}, f32[64,4,256]{2,1,0:T(4,128)S(1)}, u32[]{:S(2)}, u32[]{:S(2)}) collective-permute-start(f32[64,4,256]{2,1,0:T(4,128)S(1)} %get-tuple-element.113), channel_id=1, source_target_pairs={{0,16},{16,32},{32,48},{48,64},{64,80},{80,96},{96,112},{112,128},... | collective-permute-start | bytes 786440 | tf_op jit(solution)/shard_map/ppermute | solution.py:19
  13.0 0.7 copy-start.1
  29.2 22.3 %collective-permute-start.6 = (f32[64,8,256]{2,1,0:T(8,128)S(1)}, f32[64,8,256]{2,1,0:T(8,128)S(1)}, u32[]{:S(2)}, u32[]{:S(2)}) collective-permute-start(f32[64,8,256]{2,1,0:T(8,128)S(1)} %get-tuple-element.6), channel_id=1, source_target_pairs={{1,0},{2,1},{3,2},{4,3},{5,4},{6,5},{7,6},{8,7},{9,8},{10,9},{11,1... | collective-permute-start | bytes 1572872 | tf_op jit(solution)/shard_map/ppermute | solution.py:20
  30.7 20.9 %collective-permute-start.7 = (f32[64,8,256]{2,1,0:T(8,128)S(1)}, f32[64,8,256]{2,1,0:T(8,128)S(1)}, u32[]{:S(2)}, u32[]{:S(2)}) collective-permute-start(f32[64,8,256]{2,1,0:T(8,128)S(1)} %get-tuple-element.6), channel_id=1, source_target_pairs={{0,1},{1,2},{2,3},{3,4},{4,5},{5,6},{6,7},{7,8},{8,9},{9,10},{10,1... | collective-permute-start | bytes 1572872 | tf_op jit(solution)/shard_map/ppermute | solution.py:19
  31.0 10.0 %collective-permute-start.4 = (f32[64,4,256]{2,1,0:T(4,128)S(1)}, f32[64,4,256]{2,1,0:T(4,128)S(1)}, u32[]{:S(2)}, u32[]{:S(2)}) collective-permute-start(f32[64,4,256]{2,1,0:T(4,128)S(1)} %get-tuple-element.75), channel_id=1, source_target_pairs={{16,0},{32,16},{48,32},{64,48},{80,64},{96,80},{112,96},{128,112},... | collective-permute-start | bytes 786440 | tf_op jit(solution)/shard_map/ppermute | solution.py:20
  37.1 14.5 %collective-permute-start.5 = (f32[64,4,256]{2,1,0:T(4,128)S(1)}, f32[64,4,256]{2,1,0:T(4,128)S(1)}, u32[]{:S(2)}, u32[]{:S(2)}) collective-permute-start(f32[64,4,256]{2,1,0:T(4,128)S(1)} %get-tuple-element.76), channel_id=1, source_target_pairs={{0,16},{16,32},{32,48},{48,64},{64,80},{80,96},{96,112},{112,128},... | collective-permute-start | bytes 786440 | tf_op jit(solution)/shard_map/ppermute | solution.py:19
  56.6 23.4 %collective-permute-start.10 = (f32[64,8,256]{2,1,0:T(8,128)S(1)}, f32[64,8,256]{2,1,0:T(8,128)S(1)}, u32[]{:S(2)}, u32[]{:S(2)}) collective-permute-start(f32[64,8,256]{2,1,0:T(8,128)S(1)} %fusion.33), channel_id=1, source_target_pairs={{1,0},{2,1},{3,2},{4,3},{5,4},{6,5},{7,6},{8,7},{9,8},{10,9},{11,1... | collective-permute-start | bytes 1572872 | tf_op jit(solution)/shard_map/ppermute | solution.py:20
  57.9 22.1 %collective-permute-start.11 = (f32[64,8,256]{2,1,0:T(8,128)S(1)}, f32[64,8,256]{2,1,0:T(8,128)S(1)}, u32[]{:S(2)}, u32[]{:S(2)}) collective-permute-start(f32[64,8,256]{2,1,0:T(8,128)S(1)} %fusion.33), channel_id=1, source_target_pairs={{0,1},{1,2},{2,3},{3,4},{4,5},{5,6},{6,7},{7,8},{8,9},{9,10},{10,1... | collective-permute-start | bytes 1572872 | tf_op jit(solution)/shard_map/ppermute | solution.py:19
  59.5 8.1 %collective-permute-start.8 = (f32[64,4,256]{2,1,0:T(4,128)S(1)}, f32[64,4,256]{2,1,0:T(4,128)S(1)}, u32[]{:S(2)}, u32[]{:S(2)}) collective-permute-start(f32[64,4,256]{2,1,0:T(4,128)S(1)} %get-tuple-element.41), channel_id=1, source_target_pairs={{16,0},{32,16},{48,32},{64,48},{80,64},{96,80},{112,96},{128,112},... | collective-permute-start | bytes 786440 | tf_op jit(solution)/shard_map/ppermute | solution.py:20
  64.2 15.7 %collective-permute-start.9 = (f32[64,4,256]{2,1,0:T(4,128)S(1)}, f32[64,4,256]{2,1,0:T(4,128)S(1)}, u32[]{:S(2)}, u32[]{:S(2)}) collective-permute-start(f32[64,4,256]{2,1,0:T(4,128)S(1)} %get-tuple-element.42), channel_id=1, source_target_pairs={{0,16},{16,32},{32,48},{48,64},{64,80},{80,96},{96,112},{112,128},... | collective-permute-start | bytes 786440 | tf_op jit(solution)/shard_map/ppermute | solution.py:19
where the time goes:
time: 263 us
  blocking collectives  151 us (57%)
  waiting for transfers between devices  38.5 us (15%)
  other arithmetic  35 us (13%)
  starting transfers between devices  23.7 us (9%)
  local copies, waits for them, and re-layouts  11.6 us (4%)
    psum x2, blocking collectives, orthonormal(): total_gram = lax.psum(local_gram, ('gx', 'gy'))  151 us
    ppermute x6, waiting for transfers between devices, padded(): before = lax.ppermute(last, axis, up)  25.9 us
    ppermute x6, starting transfers between devices, padded(): after = lax.ppermute(first, axis, down)  20.2 us
    another operation x6, other arithmetic, orthonormal(): lower_factor = jnp.linalg.cholesky(total_gram)  13 us
    ppermute x6, waiting for transfers between devices, padded(): after = lax.ppermute(first, axis, down)  12.5 us
    another operation x4, other arithmetic, orthonormal(): lax.linalg.triangular_solve(lower_factor, matrix, left_side=True, lower=T...  11.1 us
  transfers between devices with their start and end apart: 12, of which 6 were waited for; matrix products, arithmetic and copies ran while one was open for 2% of the time, Pallas kernels for 0%

commit v1 on v0

--- a/solution.py
+++ b/solution.py
@@ -2,6 +2,7 @@
 import jax.numpy as jnp
 from jax import lax
 from jax.sharding import PartitionSpec as P
+from jax.lax import all_gather
 
 NZ = 64
 COEFS = (-205.0 / 72.0, 8.0 / 5.0, -1.0 / 5.0, 8.0 / 315.0, -1.0 / 560.0)
@@ -59,7 +60,7 @@
 
 def orthonormal(matrix, ncount):
     local_gram = jnp.dot(matrix, matrix.T, precision=lax.Precision.HIGHEST) / ncount
-    total_gram = lax.psum(local_gram, ("gx", "gy"))
+    total_gram = all_gather(local_gram, axis_name=("gx", "gy")).sum(axis=0)
     lower_factor = jnp.linalg.cholesky(total_gram)
     return lax.linalg.triangular_solve(lower_factor, matrix, left_side=True, lower=True)
 

time: 263 us -> 970 us (3.69)
  waiting for transfers between devices: 38.5 us -> 869 us
  blocking collectives: 151 us -> 0 us
  between operations: 0.39 us -> 13.8 us
    all_gather x0 -> x2, waiting for transfers between devices: none -> 835 us  [orthonormal(): total_gram = all_gather(local_gram, axis_name=('gx', 'gy')).sum(axis=0)]
    psum x2 -> x0, blocking collectives: 151 us -> none  [orthonormal(): total_gram = lax.psum(local_gram, ('gx', 'gy'))]
  transfers between devices with their start and end apart: 12 -> 14, of which waited for: 6 -> 8; matrix products, arithmetic and copies ran while one was open for 2% -> 1% of each run, Pallas kernels for 0% -> 0%
where the time goes in v1:
time: 970 us; the launch traced here: 969 us
  waiting for transfers between devices  869 us (90%)
  other arithmetic  43 us (4%)
  starting transfers between devices  24 us (2%)
  local copies, waits for them, and re-layouts  15.9 us (2%)
  between operations  13.8 us (1%)
    all_gather x2, waiting for transfers between devices, orthonormal(): total_gram = all_gather(local_gram, axis_name=('gx', 'gy')).sum(axis=0)  835 us
    ppermute x6, waiting for transfers between devices, padded(): before = lax.ppermute(last, axis, up)  25.9 us
    ppermute x6, starting transfers between devices, padded(): after = lax.ppermute(first, axis, down)  20.2 us
  transfers between devices with their start and end apart: 14, of which 8 were waited for; matrix products, arithmetic and copies ran while one was open for 1% of the time, Pallas kernels for 0%

profile of v1, /device:TPU:1, one launch (start us, length us, event | category | flops | bytes accessed | tf_op | source)
XLA Modules:
  0.0 969.5 jit_solution(15425333245427688819)
XLA Ops:
  6.5 2.6 collective-permute-start.3
  11.1 6.0 collective-permute-start
  18.5 1.4 fusion.194
  20.0 1.4 fusion.197
  25.0 1.8 collective-permute-done
  27.0 3.0 collective-permute-done.1
  30.0 3.3 broadcast_multiply_fusion
  35.7 1.5 collective-permute-start.6
  37.6 6.1 collective-permute-start.4
  44.1 3.5 collective-permute-done.4
  47.6 10.5 %collective-permute-done.5 = f32[64,4,256]{2,1,0:T(4,128)S(1)} collective-permute-done((f32[64,4,256]{2,1,0:T(4,128)S(1)}, f32[64,4,256]{2,1,0:T(4,128)S(1)}, u32[]{:S(2)}, u32[]{:S(2)}) %collective-permute-start.5) | collective-permute-done | bytes 262176 | tf_op jit(solution)/shard_map/ppermute | solution.py:20
  58.1 3.7 fusion.33
  66.1 4.7 collective-permute-start.8
  71.2 3.0 collective-permute-done.8
  74.2 12.4 %collective-permute-done.9 = f32[64,4,256]{2,1,0:T(4,128)S(1)} collective-permute-done((f32[64,4,256]{2,1,0:T(4,128)S(1)}, f32[64,4,256]{2,1,0:T(4,128)S(1)}, u32[]{:S(2)}, u32[]{:S(2)}) %collective-permute-start.9) | collective-permute-done | bytes 262176 | tf_op jit(solution)/shard_map/ppermute | solution.py:20
  86.5 3.7 fusion.13
  92.0 417.7 %all-gather.5.cloned.1.call-done = f32[16384,64]{1,0:T(8,128)} async-done(((f32[64,64]{1,0:T(8,128)}), f32[16384,64]{1,0:T(8,128)}) %all-gather.5.cloned.1.call-update) | async-done | bytes 4194320 | tf_op jit(solution)/shard_map/all_gather | solution.py:63
  509.8 4.0 reduce_sum.18
  513.9 5.8 cholesky.44
  521.0 4.9 custom-call.6
  527.8 417.0 %all-gather.7.cloned.1.call-done = f32[16384,64]{1,0:T(8,128)} async-done(((f32[64,64]{1,0:T(8,128)}), f32[16384,64]{1,0:T(8,128)}) %all-gather.7.cloned.1.call-update) | async-done | bytes 4194320 | tf_op jit(solution)/shard_map/all_gather | solution.py:63
  944.8 4.0 reduce_sum.19
  948.9 5.8 cholesky.55
  956.1 4.9 custom-call.7
  (95 shorter events, 22.7 us)
Async XLA Ops:
  6.5 16.3 %copy-start = (f32[64,8,256]{2,1,0:T(8,128)S(1)}, f32[64,8,256]{2,1,0:T(8,128)}, u32[]{:S(2)}) copy-start(f32[64,8,256]{2,1,0:T(8,128)} %param.5) | copy-start | bytes 1572868
  6.5 503.2 %all-gather.5.cloned.1.call-start = ((), (), s32[]{:S(2)}) async-start(), calls=%async_computation | async-start | bytes 8421376 | tf_op jit(solution)/shard_map/all_gather | solution.py:63
  6.5 18.2 %collective-permute-start.3 = (f32[64,8,256]{2,1,0:T(8,128)}, f32[64,8,256]{2,1,0:T(8,128)S(1)}, u32[]{:S(2)}, u32[]{:S(2)}) collective-permute-start(f32[64,8,256]{2,1,0:T(8,128)} %param.5), channel_id=1, source_target_pairs={{0,1},{1,2},{2,3},{3,4},{4,5},{5,6},{6,7},{7,8},{8,9},{9,10},{10,1... | collective-permute-start | bytes 1572872 | tf_op jit(solution)/shard_map/ppermute | solution.py:20
  9.1 17.8 %collective-permute-start.2 = (f32[64,8,256]{2,1,0:T(8,128)}, f32[64,8,256]{2,1,0:T(8,128)S(1)}, u32[]{:S(2)}, u32[]{:S(2)}) collective-permute-start(f32[64,8,256]{2,1,0:T(8,128)} %param.5), channel_id=1, source_target_pairs={{1,0},{2,1},{3,2},{4,3},{5,4},{6,5},{7,6},{8,7},{9,8},{10,9},{11,1... | collective-permute-start | bytes 1572872 | tf_op jit(solution)/shard_map/ppermute | solution.py:21
  11.1 15.7 %collective-permute-start = (f32[64,4,256]{2,1,0:T(4,128)S(1)}, f32[64,4,256]{2,1,0:T(4,128)S(1)}, u32[]{:S(2)}, u32[]{:S(2)}) collective-permute-start(f32[64,4,256]{2,1,0:T(4,128)S(1)} %get-tuple-element.112), channel_id=1, source_target_pairs={{16,0},{32,16},{48,32},{64,48},{80,64},{96,80},{112,96},{128,112},... | collective-permute-start | bytes 786440 | tf_op jit(solution)/shard_map/ppermute | solution.py:21
  17.1 12.9 %collective-permute-start.1 = (f32[64,4,256]{2,1,0:T(4,128)S(1)}, f32[64,4,256]{2,1,0:T(4,128)S(1)}, u32[]{:S(2)}, u32[]{:S(2)}) collective-permute-start(f32[64,4,256]{2,1,0:T(4,128)S(1)} %get-tuple-element.113), channel_id=1, source_target_pairs={{0,16},{16,32},{32,48},{48,64},{64,80},{80,96},{96,112},{112,128},... | collective-permute-start | bytes 786440 | tf_op jit(solution)/shard_map/ppermute | solution.py:20
  21.4 3.1 copy-start.1
  35.7 22.4 %collective-permute-start.6 = (f32[64,8,256]{2,1,0:T(8,128)S(1)}, f32[64,8,256]{2,1,0:T(8,128)S(1)}, u32[]{:S(2)}, u32[]{:S(2)}) collective-permute-start(f32[64,8,256]{2,1,0:T(8,128)S(1)} %get-tuple-element.6), channel_id=1, source_target_pairs={{1,0},{2,1},{3,2},{4,3},{5,4},{6,5},{7,6},{8,7},{9,8},{10,9},{11,1... | collective-permute-start | bytes 1572872 | tf_op jit(solution)/shard_map/ppermute | solution.py:21
  37.2 20.9 %collective-permute-start.7 = (f32[64,8,256]{2,1,0:T(8,128)S(1)}, f32[64,8,256]{2,1,0:T(8,128)S(1)}, u32[]{:S(2)}, u32[]{:S(2)}) collective-permute-start(f32[64,8,256]{2,1,0:T(8,128)S(1)} %get-tuple-element.6), channel_id=1, source_target_pairs={{0,1},{1,2},{2,3},{3,4},{4,5},{5,6},{6,7},{7,8},{8,9},{9,10},{10,1... | collective-permute-start | bytes 1572872 | tf_op jit(solution)/shard_map/ppermute | solution.py:20
  37.6 10.0 %collective-permute-start.4 = (f32[64,4,256]{2,1,0:T(4,128)S(1)}, f32[64,4,256]{2,1,0:T(4,128)S(1)}, u32[]{:S(2)}, u32[]{:S(2)}) collective-permute-start(f32[64,4,256]{2,1,0:T(4,128)S(1)} %get-tuple-element.75), channel_id=1, source_target_pairs={{16,0},{32,16},{48,32},{64,48},{80,64},{96,80},{112,96},{128,112},... | collective-permute-start | bytes 786440 | tf_op jit(solution)/shard_map/ppermute | solution.py:21
  43.7 14.5 %collective-permute-start.5 = (f32[64,4,256]{2,1,0:T(4,128)S(1)}, f32[64,4,256]{2,1,0:T(4,128)S(1)}, u32[]{:S(2)}, u32[]{:S(2)}) collective-permute-start(f32[64,4,256]{2,1,0:T(4,128)S(1)} %get-tuple-element.76), channel_id=1, source_target_pairs={{0,16},{16,32},{32,48},{48,64},{64,80},{80,96},{96,112},{112,128},... | collective-permute-start | bytes 786440 | tf_op jit(solution)/shard_map/ppermute | solution.py:20
  63.2 23.4 %collective-permute-start.10 = (f32[64,8,256]{2,1,0:T(8,128)S(1)}, f32[64,8,256]{2,1,0:T(8,128)S(1)}, u32[]{:S(2)}, u32[]{:S(2)}) collective-permute-start(f32[64,8,256]{2,1,0:T(8,128)S(1)} %fusion.33), channel_id=1, source_target_pairs={{1,0},{2,1},{3,2},{4,3},{5,4},{6,5},{7,6},{8,7},{9,8},{10,9},{11,1... | collective-permute-start | bytes 1572872 | tf_op jit(solution)/shard_map/ppermute | solution.py:21
  64.4 22.1 %collective-permute-start.11 = (f32[64,8,256]{2,1,0:T(8,128)S(1)}, f32[64,8,256]{2,1,0:T(8,128)S(1)}, u32[]{:S(2)}, u32[]{:S(2)}) collective-permute-start(f32[64,8,256]{2,1,0:T(8,128)S(1)} %fusion.33), channel_id=1, source_target_pairs={{0,1},{1,2},{2,3},{3,4},{4,5},{5,6},{6,7},{7,8},{8,9},{9,10},{10,1... | collective-permute-start | bytes 1572872 | tf_op jit(solution)/shard_map/ppermute | solution.py:20
  66.1 8.1 collective-permute-start.8
  70.8 15.7 %collective-permute-start.9 = (f32[64,4,256]{2,1,0:T(4,128)S(1)}, f32[64,4,256]{2,1,0:T(4,128)S(1)}, u32[]{:S(2)}, u32[]{:S(2)}) collective-permute-start(f32[64,4,256]{2,1,0:T(4,128)S(1)} %get-tuple-element.42), channel_id=1, source_target_pairs={{0,16},{16,32},{32,48},{48,64},{64,80},{80,96},{96,112},{112,128},... | collective-permute-start | bytes 786440 | tf_op jit(solution)/shard_map/ppermute | solution.py:20
  91.6 853.2 %all-gather.7.cloned.1.call-start = ((), (), s32[]{:S(2)}) async-start(), calls=%async_computation.1 | async-start | bytes 8421376 | tf_op jit(solution)/shard_map/all_gather | solution.py:63
Sparse Core Ops, SparseCore 0:
  91.7 417.9 all-gather.4
  527.9 416.8 all-gather.6
